TPU v7x, 32 devices: a whole 2x2x4 slice. The times are simulated.
32 devices in a mesh: dp: 8 (over z, x), expert: 4 (over y, core).
Axes of the slice: x: 2, y: 2, z: 4, core: 2. Of those that a mesh axis runs over, the one named last changes fastest.
Arguments:
- tokens: bfloat16 [8192, 768], P(('dp', 'expert')), may hold values from -6 to 6
- expert_ids: int32 [8192, 2], P(('dp', 'expert')), may hold values from 0 to 15, all different within a row; in each aligned block of 256 rows (0 to 255, 256 to 511, ...) at most 64 rows name the same one
- gate_fixed: int32 [8192, 2], P(('dp', 'expert')), may hold values from 8192 to 65535
- cotangent: bfloat16 [8192, 768], P(('dp', 'expert')), may hold values from -6 to 6
- w_gate: bfloat16 [16, 768, 384], P('expert'), may hold values from -0.21875 to 0.21875
- w_up: bfloat16 [16, 768, 384], P('expert'), may hold values from -0.21875 to 0.21875
- w_down: bfloat16 [16, 768, 384], P('expert'), may hold values from -0.3125 to 0.3125
Outputs:
- layer_out: bfloat16 [8192, 768], P(('dp', 'expert'))
- input_grad: bfloat16 [8192, 768], P(('dp', 'expert'))
- grad_gate: float32 [16, 768, 384], P('expert', 'dp')
- grad_up: float32 [16, 768, 384], P('expert', 'dp')
- grad_down: float32 [16, 768, 384], P('expert', 'dp')
Inputs may be any that keep to these rules, and one draw needn't show every extreme that they name: `expert_ids`: A row names 2 different experts. In each aligned block of 256 rows (the rows of one device) no expert is named by more than 64 rows, and in some block one expert is named by exactly 64 rows.
All inputs are finite; a program needn't handle non-finite values.
Results may differ from a plain program's by a relative error of at most 0.015.
Values may be sent and summed in bfloat16 or wider, within the bound.
A program may use at most 64 MiB of HBM per device.

v0:
```python
import jax
import jax.numpy as jnp
from jax import lax
from jax.sharding import PartitionSpec as P


def expert_forward(rows_in, w_gate, w_up, w_down):
    pre_gate = jnp.einsum("erd,edf->erf", rows_in, w_gate, preferred_element_type=jnp.float32)
    pre_up = jnp.einsum("erd,edf->erf", rows_in, w_up, preferred_element_type=jnp.float32)
    sigmoid_gate = jax.nn.sigmoid(pre_gate)
    activated = pre_gate * sigmoid_gate
    hidden = (activated * pre_up).astype(jnp.bfloat16)
    outputs = jnp.einsum("erf,edf->erd", hidden, w_down, preferred_element_type=jnp.float32).astype(
        jnp.bfloat16
    )
    return (outputs, (pre_gate, pre_up, sigmoid_gate, activated, hidden))


def expert_backward(rows_in, grads_in, saved_state, w_gate, w_up, w_down, grad_scale):
    pre_gate, pre_up, sigmoid_gate, activated, hidden = saved_state
    hidden_grad = jnp.einsum("erd,edf->erf", grads_in, w_down, preferred_element_type=jnp.float32)
    gate_grad = (
        hidden_grad * pre_up * sigmoid_gate * (1.0 + pre_gate * (1.0 - sigmoid_gate))
    ).astype(jnp.bfloat16)
    up_grad = (hidden_grad * activated).astype(jnp.bfloat16)
    entry_grad = (
        jnp.einsum("erf,edf->erd", gate_grad, w_gate, preferred_element_type=jnp.float32)
        + jnp.einsum("erf,edf->erd", up_grad, w_up, preferred_element_type=jnp.float32)
    ).astype(jnp.bfloat16)
    weight_gate = (
        jnp.einsum("erd,erf->edf", rows_in, gate_grad, preferred_element_type=jnp.float32)
        * grad_scale
    )
    weight_up = (
        jnp.einsum("erd,erf->edf", rows_in, up_grad, preferred_element_type=jnp.float32)
        * grad_scale
    )
    weight_down = (
        jnp.einsum("erd,erf->edf", grads_in, hidden, preferred_element_type=jnp.float32)
        * grad_scale
    )
    return (entry_grad, weight_gate, weight_up, weight_down)


def shards(tokens, expert_ids, gate_fixed, cotangent, w_gate, w_up, w_down):
    peer_count = lax.axis_size("expert")
    replicas = lax.axis_size("dp")
    local_experts = w_gate.shape[0]
    tok_rows = expert_ids.shape[0]
    top_count = expert_ids.shape[1]
    d_model = tokens.shape[1]
    experts_all = local_experts * peer_count
    entries = tok_rows * top_count
    capacity = entries * 2 // experts_all
    slots_all = experts_all * capacity
    grad_scale = float(tok_rows * replicas * top_count // local_experts) ** (-0.5)
    flat_ids = expert_ids.reshape(entries)
    onehot = (flat_ids[:, None] == jnp.arange(experts_all, dtype=jnp.int32)[None, :]).astype(
        jnp.int32
    )
    slot_rank = jnp.sum((jnp.cumsum(onehot, axis=0) - 1) * onehot, axis=1)
    owner_dev = flat_ids // local_experts
    within = flat_ids % local_experts
    slot_index = (within * peer_count + owner_dev) * capacity + slot_rank
    source = (
        jnp.full((slots_all,), entries, jnp.int32)
        .at[slot_index]
        .set(jnp.arange(entries, dtype=jnp.int32))
    )
    is_valid = source < entries
    token_of = jnp.where(is_valid, source // top_count, 0)
    gate_values = gate_fixed.reshape(entries).astype(jnp.float32) / 65536.0
    slot_gate = jnp.where(is_valid, gate_values[jnp.minimum(source, entries - 1)], 0.0)
    send_rows = jnp.where(is_valid[:, None], tokens[token_of], jnp.zeros((), jnp.bfloat16))
    send_rows = send_rows.reshape(local_experts, peer_count * capacity, d_model)
    send_grads = (slot_gate[:, None] * cotangent[token_of].astype(jnp.float32)).astype(jnp.bfloat16)
    send_grads = send_grads.reshape(local_experts, peer_count * capacity, d_model)
    rows_in = lax.all_to_all(send_rows, "expert", split_axis=1, concat_axis=1, tiled=True)
    outputs, saved_state = expert_forward(rows_in, w_gate, w_up, w_down)
    back_out = lax.all_to_all(outputs, "expert", split_axis=1, concat_axis=1, tiled=True)
    grads_in = lax.all_to_all(send_grads, "expert", split_axis=1, concat_axis=1, tiled=True)
    entry_grad, weight_gate, weight_up, weight_down = expert_backward(
        rows_in, grads_in, saved_state, w_gate, w_up, w_down, grad_scale
    )
    back_in = lax.all_to_all(entry_grad, "expert", split_axis=1, concat_axis=1, tiled=True)

    def combine(returned, weights):
        picked = returned.reshape(slots_all, d_model)[slot_index].astype(jnp.float32)
        summed = jnp.sum((weights[:, None] * picked).reshape(tok_rows, top_count, d_model), axis=1)
        return summed.astype(jnp.bfloat16)

    layer_out = combine(back_out, gate_values)
    input_grad = combine(back_in, jnp.ones_like(gate_values))
    grad_gate, grad_up, grad_down = (
        lax.psum_scatter(
            weight_gate.astype(jnp.bfloat16), "dp", scatter_dimension=1, tiled=True
        ).astype(jnp.float32),
        lax.psum_scatter(
            weight_up.astype(jnp.bfloat16), "dp", scatter_dimension=1, tiled=True
        ).astype(jnp.float32),
        lax.psum_scatter(
            weight_down.astype(jnp.bfloat16), "dp", scatter_dimension=1, tiled=True
        ).astype(jnp.float32),
    )
    return (layer_out, input_grad, grad_gate, grad_up, grad_down)


def solution(mesh):
    return jax.shard_map(
        shards,
        mesh=mesh,
        in_specs=(
            P(("dp", "expert"), None),
            P(("dp", "expert"), None),
            P(("dp", "expert"), None),
            P(("dp", "expert"), None),
            P("expert", None, None),
            P("expert", None, None),
            P("expert", None, None),
        ),
        out_specs=(
            P(("dp", "expert"), None),
            P(("dp", "expert"), None),
            P("expert", "dp", None),
            P("expert", "dp", None),
            P("expert", "dp", None),
        ),
        check_vma=False,
    )
```

profile of v0, /device:TPU:0, one launch (start us, length us, event | category | flops | bytes accessed | tf_op | source)
XLA Modules:
  0.0 315.9 jit_solution(13793462235881466038)
XLA Ops:
  7.2 0.0 copy-start
  7.2 1.0 copy.44
  8.1 0.1 eq.31
  8.3 0.1 eq.27
  8.4 0.1 reshape.196
  8.6 0.7 convert_multiply_fusion
  9.3 0.1 copy.43
  9.4 0.1 div.43
  9.6 1.2 reduce-window.6
  10.7 0.2 slice_reduce_fusion
  11.0 0.1 fusion.3
  11.1 2.4 scatter_custom_fusion
  13.6 0.0 copy-start.1
  13.6 6.9 %gather_fusion.2 = f32[1024]{0:T(1024)S(1)} fusion(f32[512]{0:T(512)S(1)} %div.43, s32[1024]{0:T(1024)S(1)} %fusion.8), kind=kCustom, calls=%fused_computation.2 | custom fusion | bytes 12288 | tf_op jit(solution)/shard_map/gather | solution.py:73
  20.5 0.2 copy.48
  20.7 0.0 copy-done.1
  20.7 5.2 %gather_fusion = bf16[1024,768]{1,0:T(8,128)(2,1)} fusion(bf16[256,768]{1,0:T(8,128)(2,1)S(1)} %copy-done.1, s32[1024]{0:T(1024)S(1)} %fusion.7), kind=kCustom, calls=%fused_computation | custom fusion | bytes 3149824 | tf_op jit(solution)/shard_map/gather | solution.py:74
  25.9 3.8 %copy_select_fusion = bf16[4,256,768]{2,0,1:T(4,128)(2,1)} fusion(bf16[4,256,768]{2,1,0:T(8,128)(2,1)} %bitcast.43, pred[4,256]{0,1:T(8,128)(4,1)S(1)} %copy.48), kind=kLoop, calls=%fused_computation.13 | loop fusion | flops 786432 | bytes 3146752 | tf_op jit(solution)/shard_map/jit(_where)/select_n | solution.py:74
  29.8 4.5 %all-to-all-start = ((bf16[4,256,768]{2,0,1:T(4,128)(2,1)}), bf16[4,256,768]{2,0,1:T(4,128)(2,1)}, u32[]{:S(2)}, u32[]{:S(2)}) async-start(bf16[4,256,768]{2,0,1:T(4,128)(2,1)} %copy_select_fusion), calls=%async_computation | async-start | bytes 3145728 | tf_op jit(solution)/shard_map/all_to_all | solution.py:78
  34.3 0.1 copy.55
  34.4 5.2 %gather_fusion.3 = bf16[1024,768]{1,0:T(8,128)(2,1)} fusion(bf16[256,768]{1,0:T(8,128)(2,1)S(1)} %copy-done.2, s32[1024]{0:T(1024)S(1)} %fusion.7), kind=kCustom, calls=%fused_computation.3 | custom fusion | bytes 3149824 | tf_op jit(solution)/shard_map/gather | solution.py:76
  39.6 1.7 convert.3
  41.3 3.2 %fusion = bf16[4,256,768]{2,0,1:T(4,128)(2,1)} fusion(f32[4,256,768]{2,1,0:T(8,128)S(1)} %convert.3, f32[4,256]{0,1:T(8,128)S(1)} %copy.55), kind=kLoop, calls=%fused_computation.10 | loop fusion | flops 1572864 | bytes 4722688 | tf_op jit(solution)/shard_map/convert_element_type | solution.py:76
  44.6 10.6 %all-to-all-done = bf16[4,256,768]{2,0,1:T(4,128)(2,1)} async-done(((bf16[4,256,768]{2,0,1:T(4,128)(2,1)}), bf16[4,256,768]{2,0,1:T(4,128)(2,1)}, u32[]{:S(2)}, u32[]{:S(2)}) %all-to-all-start) | async-done | bytes 1572896 | tf_op jit(solution)/shard_map/all_to_all | solution.py:78
  55.1 4.3 %all-to-all-start.2 = ((bf16[4,256,768]{2,0,1:T(4,128)(2,1)}), bf16[4,256,768]{2,0,1:T(4,128)(2,1)}, u32[]{:S(2)}, u32[]{:S(2)}) async-start(bf16[4,256,768]{2,0,1:T(4,128)(2,1)} %fusion), calls=%async_computation.2 | async-start | bytes 3145728 | tf_op jit(solution)/shard_map/all_to_all | solution.py:81
  59.4 0.2 reduce-scatter.8.cloned.1.call-start
  59.7 3.8 %copy.60 = bf16[4,256,768]{1,2,0:T(8,128)(2,1)} copy(bf16[4,256,768]{2,0,1:T(4,128)(2,1)} %all-to-all-done) | data formatting | bytes 3145728 | tf_op jit(solution)/shard_map/all_to_all | solution.py:78
  63.4 4.5 %fusion.15 = f32[4,256,384]{2,1,0:T(8,128)} fusion(bf16[4,256,768]{1,2,0:T(8,128)(2,1)} %copy.60, bf16[4,768,384]{2,1,0:T(8,128)(2,1)} %param.12), kind=kOutput, calls=%fused_computation.55 | convolution fusion | flops 603979776 | bytes 5505024 | tf_op jit(solution)/shard_map/erd,edf->erf/dot_general | solution.py:9
  67.9 2.2 fusion.14
  70.1 9.4 %all-to-all-done.2 = bf16[4,256,768]{2,0,1:T(4,128)(2,1)} async-done(((bf16[4,256,768]{2,0,1:T(4,128)(2,1)}), bf16[4,256,768]{2,0,1:T(4,128)(2,1)}, u32[]{:S(2)}, u32[]{:S(2)}) %all-to-all-start.2) | async-done | bytes 1572896 | tf_op jit(solution)/shard_map/all_to_all | solution.py:81
  79.6 3.8 %copy.62 = bf16[4,256,768]{1,2,0:T(8,128)(2,1)} copy(bf16[4,256,768]{2,0,1:T(4,128)(2,1)} %all-to-all-done.2) | data formatting | bytes 3145728 | tf_op jit(solution)/shard_map/all_to_all | solution.py:81
  83.3 4.8 %multiply_convert_fusion.3 = (bf16[4,256,384]{2,1,0:T(8,128)(2,1)}, bf16[4,256,384]{2,1,0:T(8,128)(2,1)S(1)}, bf16[4,256,384]{2,1,0:T(8,128)(2,1)S(1)}) fusion(f32[4,256,384]{2,1,0:T(8,128)} %fusion.14, f32[4,256,384]{2,1,0:T(8,128)} %fusion.15, bf16[4,256,768]{1,2,0:T(8,128)(2,1)} %copy.62, bf16[4,768,384]{2,1,0:T(8,128)(2,1)S(1)} %copy-done), kind=kOutput, calls=%fused_computation.14 | convolution fusion | flops 609878016 | bytes 9437184 | tf_op jit(solution)/shard_map/erd,edf->erf/dot_general | solution.py:21
  88.2 1.0 copy-done.7
  89.2 2.4 multiply_convert_fusion
  91.6 0.0 reduce-scatter.8.cloned.1.call-update
  91.6 0.0 reduce-scatter.6.cloned.1.call-start
  91.7 4.0 %multiply_convert_fusion.1 = bf16[4,768,384]{2,1,0:T(8,128)(2,1)} fusion(bf16[4,256,768]{1,2,0:T(8,128)(2,1)} %copy.60, bf16[4,256,384]{2,1,0:T(8,128)(2,1)} %get-tuple-element.7), kind=kOutput, calls=%fused_computation.7 | convolution fusion | flops 606339072 | bytes 4718592 | tf_op jit(solution)/shard_map/erd,erf->edf/dot_general | solution.py:35
  95.6 0.0 reduce-scatter.6.cloned.1.call-update
  95.7 0.0 reduce-scatter.4.cloned.1.call-start
  95.7 3.8 %multiply_convert_fusion.2 = bf16[4,768,384]{2,1,0:T(8,128)(2,1)} fusion(bf16[4,256,768]{1,2,0:T(8,128)(2,1)} %copy.60, bf16[4,256,384]{2,1,0:T(8,128)(2,1)S(1)} %get-tuple-element.8), kind=kOutput, calls=%fused_computation.8 | convolution fusion | flops 606339072 | bytes 4718592 | tf_op jit(solution)/shard_map/erd,erf->edf/dot_general | solution.py:31
  99.5 0.0 reduce-scatter.4.cloned.1.call-update
  99.6 2.2 convolution_convert_fusion
  101.7 2.4 copy.52
  104.1 4.4 %all-to-all-start.1 = ((bf16[4,256,768]{2,0,1:T(4,128)(2,1)}), bf16[4,256,768]{2,0,1:T(4,128)(2,1)}, u32[]{:S(2)}, u32[]{:S(2)}) async-start(bf16[4,256,768]{2,0,1:T(4,128)(2,1)} %copy.52), calls=%async_computation.1 | async-start | bytes 3145728 | tf_op jit(solution)/shard_map/all_to_all | solution.py:80
  108.5 0.0 copy-start.5
  108.5 2.8 fusion.16
  111.4 1.0 add_convert_fusion
  112.4 2.4 copy.58
  114.8 13.8 %all-to-all-done.1 = bf16[4,256,768]{2,0,1:T(4,128)(2,1)} async-done(((bf16[4,256,768]{2,0,1:T(4,128)(2,1)}), bf16[4,256,768]{2,0,1:T(4,128)(2,1)}, u32[]{:S(2)}, u32[]{:S(2)}) %all-to-all-start.1) | async-done | bytes 1572896 | tf_op jit(solution)/shard_map/all_to_all | solution.py:80
  128.6 4.6 %all-to-all-start.3 = ((bf16[4,256,768]{2,0,1:T(4,128)(2,1)}), bf16[4,256,768]{2,0,1:T(4,128)(2,1)}, u32[]{:S(2)}, u32[]{:S(2)}) async-start(bf16[4,256,768]{2,0,1:T(4,128)(2,1)} %copy.58), calls=%async_computation.3 | async-start | bytes 3145728 | tf_op jit(solution)/shard_map/all_to_all | solution.py:85
  133.2 2.9 copy.53
  136.1 4.0 %gather_fusion.1 = bf16[512,768]{1,0:T(8,128)(2,1)S(1)} fusion(bf16[1024,768]{1,0:T(8,128)(2,1)} %bitcast.42, s32[1024]{0:T(1024)S(1)} %pad_clamp_fusion), kind=kCustom, calls=%fused_computation.1 | custom fusion | bytes 1574912 | tf_op jit(solution)/shard_map/gather | solution.py:88
  140.1 2.0 reshape.200
  142.0 11.3 %all-to-all-done.3 = bf16[4,256,768]{2,0,1:T(4,128)(2,1)} async-done(((bf16[4,256,768]{2,0,1:T(4,128)(2,1)}), bf16[4,256,768]{2,0,1:T(4,128)(2,1)}, u32[]{:S(2)}, u32[]{:S(2)}) %all-to-all-start.3) | async-done | bytes 1572896 | tf_op jit(solution)/shard_map/all_to_all | solution.py:85
  153.3 2.8 copy.59
  156.1 4.7 %gather_fusion.4 = bf16[512,768]{1,0:T(8,128)(2,1)} fusion(bf16[1024,768]{1,0:T(8,128)(2,1)} %bitcast.41, s32[1024]{0:T(1024)S(1)} %pad_clamp_fusion), kind=kCustom, calls=%fused_computation.4 | custom fusion | bytes 1574912 | tf_op jit(solution)/shard_map/gather | solution.py:88
  160.8 2.2 gather.25
  162.9 2.8 reduce_sum.35
  165.8 4.2 %multiply_reduce_fusion = bf16[256,768]{1,0:T(8,128)(2,1)} fusion(f32[256,2,768]{2,1,0:T(2,128)} %reshape.200, f32[256,2]{1,0:T(8,128)S(1)} %copy.43), kind=kLoop, calls=%fused_computation.16 | loop fusion | flops 589824 | bytes 1968128 | tf_op jit(solution)/shard_map/reduce_sum | solution.py:89
  169.9 1.8 convert_element_type.88
  171.7 63.0 %reduce-scatter.6.cloned.1.call-done = bf16[4,96,384]{2,1,0:T(8,128)(2,1)} async-done(((bf16[4,768,384]{2,1,0:T(8,128)(2,1)}), bf16[4,96,384]{2,1,0:T(8,128)(2,1)}) %reduce-scatter.6.cloned.1.call-update) | async-done | bytes 294928 | tf_op jit(solution)/shard_map/reduce_scatter | solution.py:98
  234.8 1.8 convert_element_type.86
  236.6 70.9 %reduce-scatter.4.cloned.1.call-done = bf16[4,96,384]{2,1,0:T(8,128)(2,1)} async-done(((bf16[4,768,384]{2,1,0:T(8,128)(2,1)}), bf16[4,96,384]{2,1,0:T(8,128)(2,1)}) %reduce-scatter.4.cloned.1.call-update) | async-done | bytes 294928 | tf_op jit(solution)/shard_map/reduce_scatter | solution.py:95
  307.5 1.8 convert_element_type.84
  (25 shorter events, 0.2 us)
Async XLA Ops:
  7.2 76.2 %copy-start = (bf16[4,768,384]{2,1,0:T(8,128)(2,1)S(1)}, bf16[4,768,384]{2,1,0:T(8,128)(2,1)}, u32[]{:S(2)}) copy-start(bf16[4,768,384]{2,1,0:T(8,128)(2,1)} %param.13) | copy-start | bytes 7077892
  13.6 7.1 %copy-start.1 = (bf16[256,768]{1,0:T(8,128)(2,1)S(1)}, bf16[256,768]{1,0:T(8,128)(2,1)}, u32[]{:S(2)}) copy-start(bf16[256,768]{1,0:T(8,128)(2,1)} %param.7) | copy-start | bytes 1179652
  29.8 4.6 %copy-start.2 = (bf16[256,768]{1,0:T(8,128)(2,1)S(1)}, bf16[256,768]{1,0:T(8,128)(2,1)}, u32[]{:S(2)}) copy-start(bf16[256,768]{1,0:T(8,128)(2,1)} %param.10) | copy-start | bytes 1179652
  29.8 25.3 %all-to-all-start = ((bf16[4,256,768]{2,0,1:T(4,128)(2,1)}), bf16[4,256,768]{2,0,1:T(4,128)(2,1)}, u32[]{:S(2)}, u32[]{:S(2)}) async-start(bf16[4,256,768]{2,0,1:T(4,128)(2,1)} %copy_select_fusion), calls=%async_computation | async-start | bytes 3145728 | tf_op jit(solution)/shard_map/all_to_all | solution.py:78
  55.1 24.5 %all-to-all-start.2 = ((bf16[4,256,768]{2,0,1:T(4,128)(2,1)}), bf16[4,256,768]{2,0,1:T(4,128)(2,1)}, u32[]{:S(2)}, u32[]{:S(2)}) async-start(bf16[4,256,768]{2,0,1:T(4,128)(2,1)} %fusion), calls=%async_computation.2 | async-start | bytes 3145728 | tf_op jit(solution)/shard_map/all_to_all | solution.py:81
  59.4 110.5 %reduce-scatter.8.cloned.1.call-start = ((), (), s32[]{:S(2)}) async-start(), calls=%async_computation.9 | async-start | bytes 2654208 | tf_op jit(solution)/shard_map/reduce_scatter | solution.py:101
  63.4 4.5 %copy-start.3 = (bf16[4,256,768]{1,2,0:T(8,128)(2,1)S(1)}, bf16[4,256,768]{1,2,0:T(8,128)(2,1)}, u32[]{:S(2)}) copy-start(bf16[4,256,768]{1,2,0:T(8,128)(2,1)} %copy.60) | copy-start | bytes 4718596
  63.4 4.5 %copy-start.4 = (bf16[4,768,384]{2,1,0:T(8,128)(2,1)S(1)}, bf16[4,768,384]{2,1,0:T(8,128)(2,1)}, u32[]{:S(2)}) copy-start(bf16[4,768,384]{2,1,0:T(8,128)(2,1)} %param.11) | copy-start | bytes 7077892
  83.3 5.8 %copy-start.6 = (bf16[4,256,768]{1,2,0:T(8,128)(2,1)S(1)}, bf16[4,256,768]{1,2,0:T(8,128)(2,1)}, u32[]{:S(2)}) copy-start(bf16[4,256,768]{1,2,0:T(8,128)(2,1)} %copy.62) | copy-start | bytes 4718596
  88.2 1.0 copy-start.7
  91.6 143.2 %reduce-scatter.6.cloned.1.call-start = ((), (), s32[]{:S(2)}) async-start(), calls=%async_computation.8 | async-start | bytes 2654208 | tf_op jit(solution)/shard_map/reduce_scatter | solution.py:98
  95.7 211.9 %reduce-scatter.4.cloned.1.call-start = ((), (), s32[]{:S(2)}) async-start(), calls=%async_computation.7 | async-start | bytes 2654208 | tf_op jit(solution)/shard_map/reduce_scatter | solution.py:95
  104.1 24.5 %all-to-all-start.1 = ((bf16[4,256,768]{2,0,1:T(4,128)(2,1)}), bf16[4,256,768]{2,0,1:T(4,128)(2,1)}, u32[]{:S(2)}, u32[]{:S(2)}) async-start(bf16[4,256,768]{2,0,1:T(4,128)(2,1)} %copy.52), calls=%async_computation.1 | async-start | bytes 3145728 | tf_op jit(solution)/shard_map/all_to_all | solution.py:80
  108.5 2.9 copy-start.5
  108.5 2.9 copy-start.8
  128.6 24.7 %all-to-all-start.3 = ((bf16[4,256,768]{2,0,1:T(4,128)(2,1)}), bf16[4,256,768]{2,0,1:T(4,128)(2,1)}, u32[]{:S(2)}, u32[]{:S(2)}) async-start(bf16[4,256,768]{2,0,1:T(4,128)(2,1)} %copy.58), calls=%async_computation.3 | async-start | bytes 3145728 | tf_op jit(solution)/shard_map/all_to_all | solution.py:85
Sparse Core Ops, SparseCore 0:
  91.7 70.6 reduce-scatter.7
  166.0 68.7 reduce-scatter.5
  238.3 69.1 reduce-scatter.3
where the time goes:
time: 317 us; the launch traced here: 316 us
  waiting for transfers between devices  179 us (56%)
  local copies, waits for them, and re-layouts  53.7 us (17%)
  matrix products  27.8 us (9%)
  other arithmetic  23.2 us (7%)
  starting transfers between devices  18 us (6%)
  between operations  14 us (4%)
    reduce_scatter x1, waiting for transfers between devices, shards(): lax.psum_scatter(weight_gate.astype(jnp.bfloat16), 'dp', scatter_dimensio...  70.9 us
    reduce_scatter x1, waiting for transfers between devices, shards(): lax.psum_scatter(weight_up.astype(jnp.bfloat16), 'dp', scatter_dimension=...  63 us
    all_to_all x1, waiting for transfers between devices, shards(): lax.all_to_all(outputs, 'expert', split_axis=1, concat_axis=1, tiled=True)  13.8 us
    all_to_all x1, waiting for transfers between devices, shards(): lax.all_to_all(entry_grad, 'expert', split_axis=1, concat_axis=1, tiled=T...  11.3 us
    gather x3, local copies, waits for them, and re-layouts, combine(): returned.reshape(slots_all, d_model)[slot_index].astype(jnp.float32)  10.8 us
    all_to_all x1, waiting for transfers between devices, shards(): lax.all_to_all(send_rows, 'expert', split_axis=1, concat_axis=1, tiled=True)  10.6 us
    all_to_all x1, waiting for transfers between devices, shards(): lax.all_to_all(send_grads, 'expert', split_axis=1, concat_axis=1, tiled=T...  9.44 us
    reduce_sum x2, other arithmetic, combine(): jnp.sum((weights[:, None] * picked).reshape(tok_rows, top_count, d_model)...  7 us
  transfers between devices with their start and end apart: 7, of which 6 were waited for; matrix products, arithmetic and copies ran while one was open for 22% of the time, Pallas kernels for 0%

commit v1 on v0

--- a/solution.py
+++ b/solution.py
@@ -2,6 +2,17 @@
 import jax.numpy as jnp
 from jax import lax
 from jax.sharding import PartitionSpec as P
+
+
+def in_blocks(x, dim, size):
+    before, after = (x.shape[:dim], x.shape[dim + 1 :])
+    return jnp.moveaxis(x.reshape(*before, size, -1, *after), dim, 0)
+
+
+def laid_out(pieces, dim):
+    pieces = jnp.moveaxis(pieces, 0, dim)
+    lengths = pieces.shape
+    return pieces.reshape(*lengths[:dim], lengths[dim] * lengths[dim + 1], *lengths[dim + 2 :])
 
 
 def expert_forward(rows_in, w_gate, w_up, w_down):
@@ -75,7 +86,15 @@
     send_rows = send_rows.reshape(local_experts, peer_count * capacity, d_model)
     send_grads = (slot_gate[:, None] * cotangent[token_of].astype(jnp.float32)).astype(jnp.bfloat16)
     send_grads = send_grads.reshape(local_experts, peer_count * capacity, d_model)
-    rows_in = lax.all_to_all(send_rows, "expert", split_axis=1, concat_axis=1, tiled=True)
+    length, place = (lax.axis_size("expert"), lax.axis_index("expert"))
+    pieces = in_blocks(send_rows, 1, length)
+    filled = pieces
+    for step in range(1, length):
+        target, source_2 = ((place + step) % length, (place - step) % length)
+        sent = lax.dynamic_index_in_dim(pieces, target, 0)
+        other = lax.ppermute(sent, "expert", [(i, (i + step) % length) for i in range(length)])
+        filled = lax.dynamic_update_slice_in_dim(filled, other, source_2, axis=0)
+    rows_in = laid_out(filled, 1)
     outputs, saved_state = expert_forward(rows_in, w_gate, w_up, w_down)
     back_out = lax.all_to_all(outputs, "expert", split_axis=1, concat_axis=1, tiled=True)
     grads_in = lax.all_to_all(send_grads, "expert", split_axis=1, concat_axis=1, tiled=True)

time: 317 us -> 318 us (level)
  matrix products: 27.8 us -> 24.5 us
  local copies, waits for them, and re-layouts: 53.7 us -> 56.9 us
    ppermute x0 -> x3, waiting for transfers between devices: none -> 21.9 us  [shards(): lax.ppermute(sent, 'expert', [(i, (i + step) % length) for i in range(len...]
    all_to_all x1 -> x0, waiting for transfers between devices: 10.6 us -> none  [shards(): lax.all_to_all(send_rows, 'expert', split_axis=1, concat_axis=1, tiled=True)]
    all_to_all x1, waiting for transfers between devices: 9.44 us -> 0.01 us  [shards(): lax.all_to_all(send_grads, 'expert', split_axis=1, concat_axis=1, tiled=T...]
    dynamic_update_slice x0 -> x3, local copies, waits for them, and re-layouts: none -> 5.32 us  [shards(): filled = lax.dynamic_update_slice_in_dim(filled, other, source_2, axis=0)]
    ppermute x0 -> x3, starting transfers between devices: none -> 4.72 us  [shards(): lax.ppermute(sent, 'expert', [(i, (i + step) % length) for i in range(len...]
    all_to_all x1 -> x0, starting transfers between devices: 4.47 us -> none  [shards(): lax.all_to_all(send_rows, 'expert', split_axis=1, concat_axis=1, tiled=True)]
    all_to_all x1 -> x0, local copies, waits for them, and re-layouts: 3.76 us -> none  [shards(): lax.all_to_all(send_rows, 'expert', split_axis=1, concat_axis=1, tiled=True)]
  transfers between devices with their start and end apart: 7 -> 9, of which waited for: 6 -> 6; matrix products, arithmetic and copies ran while one was open for 22% -> 20% of each run, Pallas kernels for 0% -> 0%
where the time goes in v1:
time: 318 us; the launch traced here: 317 us
  waiting for transfers between devices  180 us (57%)
  local copies, waits for them, and re-layouts  56.9 us (18%)
  matrix products  24.5 us (8%)
  other arithmetic  22.5 us (7%)
  starting transfers between devices  18.5 us (6%)
  between operations  14.1 us (4%)
    reduce_scatter x1, waiting for transfers between devices, shards(): lax.psum_scatter(weight_gate.astype(jnp.bfloat16), 'dp', scatter_dimensio...  70.5 us
    reduce_scatter x1, waiting for transfers between devices, shards(): lax.psum_scatter(weight_up.astype(jnp.bfloat16), 'dp', scatter_dimension=...  62.1 us
    ppermute x3, waiting for transfers between devices, shards(): lax.ppermute(sent, 'expert', [(i, (i + step) % length) for i in range(len...  21.9 us
    all_to_all x1, waiting for transfers between devices, shards(): lax.all_to_all(outputs, 'expert', split_axis=1, concat_axis=1, tiled=True)  14.8 us
    all_to_all x1, waiting for transfers between devices, shards(): lax.all_to_all(entry_grad, 'expert', split_axis=1, concat_axis=1, tiled=T...  11 us
    gather x3, local copies, waits for them, and re-layouts, combine(): returned.reshape(slots_all, d_model)[slot_index].astype(jnp.float32)  10.9 us
    reduce_sum x2, other arithmetic, combine(): jnp.sum((weights[:, None] * picked).reshape(tok_rows, top_count, d_model)...  7 us
    gather x1, local copies, waits for them, and re-layouts, shards(): gate_values[jnp.minimum(source, entries - 1)]  6.87 us
  transfers between devices with their start and end apart: 9, of which 6 were waited for; matrix products, arithmetic and copies ran while one was open for 20% of the time, Pallas kernels for 0%

profile of v1, /device:TPU:0, one launch (start us, length us, event | category | flops | bytes accessed | tf_op | source)
XLA Modules:
  0.0 316.8 jit_solution(5948813317614649762)
XLA Ops:
  7.2 1.0 copy.42
  8.1 0.1 eq.38
  8.3 0.1 eq.34
  8.4 0.1 reshape.201
  8.6 0.7 convert_multiply_fusion
  9.3 0.1 copy.41
  9.4 0.1 div.43
  9.6 1.2 reduce-window.6
  10.7 0.2 slice_reduce_fusion
  11.0 0.1 fusion.3
  11.1 2.4 scatter_custom_fusion
  13.6 6.9 %gather_fusion.2 = f32[1024]{0:T(1024)S(1)} fusion(f32[512]{0:T(512)S(1)} %div.43, s32[1024]{0:T(1024)S(1)} %fusion.8), kind=kCustom, calls=%fused_computation.2 | custom fusion | bytes 12288 | tf_op jit(solution)/shard_map/gather | solution.py:84
  20.5 0.1 copy.49
  20.7 5.2 %gather_fusion.3 = bf16[1024,768]{1,0:T(8,128)(2,1)} fusion(bf16[256,768]{1,0:T(8,128)(2,1)S(1)} %copy-done.1, s32[1024]{0:T(1024)S(1)} %fusion.7), kind=kCustom, calls=%fused_computation.3 | custom fusion | bytes 3149824 | tf_op jit(solution)/shard_map/gather | solution.py:87
  25.9 1.7 convert.3
  27.6 3.3 %fusion = bf16[4,256,768]{2,0,1:T(4,128)(2,1)} fusion(f32[4,256,768]{2,1,0:T(8,128)S(1)} %convert.3, f32[4,256]{0,1:T(8,128)S(1)} %copy.49), kind=kLoop, calls=%fused_computation.10 | loop fusion | flops 1572864 | bytes 4722688 | tf_op jit(solution)/shard_map/convert_element_type | solution.py:87
  30.9 4.5 %all-to-all-start.1 = ((bf16[4,256,768]{2,0,1:T(4,128)(2,1)}), bf16[4,256,768]{2,0,1:T(4,128)(2,1)}, u32[]{:S(2)}, u32[]{:S(2)}) async-start(bf16[4,256,768]{2,0,1:T(4,128)(2,1)} %fusion), calls=%async_computation.1 | async-start | bytes 3145728 | tf_op jit(solution)/shard_map/all_to_all | solution.py:100
  35.4 0.1 broadcast_in_dim.34
  35.5 5.2 %gather_fusion = bf16[1024,768]{1,0:T(8,128)(2,1)} fusion(bf16[256,768]{1,0:T(8,128)(2,1)S(1)} %copy-done.2, s32[1024]{0:T(1024)S(1)} %fusion.7), kind=kCustom, calls=%fused_computation | custom fusion | bytes 3149824 | tf_op jit(solution)/shard_map/gather | solution.py:85
  40.8 1.6 broadcast_select_fusion
  42.4 0.8 dynamic-slice_bitcast_fusion
  43.2 0.5 collective-permute-start
  43.7 2.0 collective-permute-start.2
  45.7 2.3 collective-permute-start.1
  47.9 1.4 fusion.35
  49.4 14.4 %collective-permute-done = bf16[1,4,64,768]{3,2,0,1:T(8,128)(2,1)} collective-permute-done((bf16[1,4,64,768]{3,2,0,1:T(8,128)(2,1)}, bf16[1,4,64,768]{3,2,0,1:T(8,128)(2,1)}, u32[]{:S(2)}, u32[]{:S(2)}) %collective-permute-start) | collective-permute-done | bytes 393248 | tf_op jit(solution)/shard_map/ppermute | solution.py:95
  63.8 1.8 constant_dynamic-update-slice_fusion.2
  65.5 7.5 %collective-permute-done.1 = bf16[1,4,64,768]{3,2,0,1:T(8,128)(2,1)} collective-permute-done((bf16[1,4,64,768]{3,2,0,1:T(8,128)(2,1)S(1)}, bf16[1,4,64,768]{3,2,0,1:T(8,128)(2,1)}, u32[]{:S(2)}, u32[]{:S(2)}) %collective-permute-start.1) | collective-permute-done | bytes 393248 | tf_op jit(solution)/shard_map/ppermute | solution.py:95
  73.0 1.8 constant_dynamic-update-slice_fusion.1
  74.8 1.8 constant_dynamic-update-slice_fusion
  76.6 3.5 %fusion.14 = f32[4,256,384]{2,1,0:T(8,128)} fusion(bf16[4,256,768]{2,1,0:T(8,128)(2,1)} %bitcast.54, bf16[4,768,384]{2,1,0:T(8,128)(2,1)S(1)} %copy-done.5), kind=kOutput, calls=%fused_computation.60 | convolution fusion | flops 603979776 | bytes 5505024 | tf_op jit(solution)/shard_map/erd,edf->erf/dot_general | solution.py:20
  80.1 3.8 %copy.56 = bf16[4,256,768]{1,2,0:T(8,128)(2,1)} copy(bf16[4,256,768]{2,0,1:T(4,128)(2,1)} %all-to-all-done.1) | data formatting | bytes 3145728 | tf_op jit(solution)/shard_map/all_to_all | solution.py:100
  83.9 3.3 %fusion.15 = f32[4,256,384]{2,1,0:T(8,128)S(1)} fusion(bf16[4,256,768]{1,2,0:T(8,128)(2,1)} %copy.56, bf16[4,768,384]{2,1,0:T(8,128)(2,1)} %param.13), kind=kOutput, calls=%fused_computation.61 | convolution fusion | flops 603979776 | bytes 5505024 | tf_op jit(solution)/shard_map/erd,edf->erf/dot_general | solution.py:32
  87.3 2.3 multiply_convert_fusion.3
  89.6 1.0 copy-done.10
  90.5 2.4 multiply_convert_fusion
  93.0 0.2 reduce-scatter.6.cloned.1.call-start
  93.2 4.0 %multiply_convert_fusion.1 = bf16[4,768,384]{2,1,0:T(8,128)(2,1)} fusion(bf16[4,256,768]{2,1,0:T(8,128)(2,1)} %bitcast.55, bf16[4,256,384]{2,1,0:T(8,128)(2,1)} %get-tuple-element.7), kind=kOutput, calls=%fused_computation.7 | convolution fusion | flops 606339072 | bytes 4718592 | tf_op jit(solution)/shard_map/erd,erf->edf/dot_general | solution.py:46
  97.3 0.0 reduce-scatter.4.cloned.1.call-start
  97.4 3.9 %multiply_convert_fusion.2 = bf16[4,768,384]{2,1,0:T(8,128)(2,1)} fusion(bf16[4,256,768]{2,1,0:T(8,128)(2,1)} %bitcast.56, bf16[4,256,384]{2,1,0:T(8,128)(2,1)S(1)} %get-tuple-element.8), kind=kOutput, calls=%fused_computation.8 | convolution fusion | flops 606339072 | bytes 4718592 | tf_op jit(solution)/shard_map/erd,erf->edf/dot_general | solution.py:42
  101.2 2.9 convolution_convert_fusion
  104.2 2.4 copy.46
  106.6 4.4 %all-to-all-start = ((bf16[4,256,768]{2,0,1:T(4,128)(2,1)}), bf16[4,256,768]{2,0,1:T(4,128)(2,1)}, u32[]{:S(2)}, u32[]{:S(2)}) async-start(bf16[4,256,768]{2,0,1:T(4,128)(2,1)} %copy.46), calls=%async_computation | async-start | bytes 3145728 | tf_op jit(solution)/shard_map/all_to_all | solution.py:99
  111.0 1.0 fusion.16
  112.0 0.7 copy-done.6
  112.7 0.2 copy-done.8
  112.9 1.0 add_convert_fusion
  113.9 2.4 copy.52
  116.3 14.8 %all-to-all-done = bf16[4,256,768]{2,0,1:T(4,128)(2,1)} async-done(((bf16[4,256,768]{2,0,1:T(4,128)(2,1)}), bf16[4,256,768]{2,0,1:T(4,128)(2,1)}, u32[]{:S(2)}, u32[]{:S(2)}) %all-to-all-start) | async-done | bytes 1572896 | tf_op jit(solution)/shard_map/all_to_all | solution.py:99
  131.1 4.6 %all-to-all-start.2 = ((bf16[4,256,768]{2,0,1:T(4,128)(2,1)}), bf16[4,256,768]{2,0,1:T(4,128)(2,1)}, u32[]{:S(2)}, u32[]{:S(2)}) async-start(bf16[4,256,768]{2,0,1:T(4,128)(2,1)} %copy.52), calls=%async_computation.2 | async-start | bytes 3145728 | tf_op jit(solution)/shard_map/all_to_all | solution.py:104
  135.7 2.9 copy.47
  138.6 4.0 %gather_fusion.1 = bf16[512,768]{1,0:T(8,128)(2,1)S(1)} fusion(bf16[1024,768]{1,0:T(8,128)(2,1)} %bitcast.53, s32[1024]{0:T(1024)S(1)} %pad_clamp_fusion), kind=kCustom, calls=%fused_computation.1 | custom fusion | bytes 1574912 | tf_op jit(solution)/shard_map/gather | solution.py:107
  142.6 2.0 reshape.206
  144.6 11.0 %all-to-all-done.2 = bf16[4,256,768]{2,0,1:T(4,128)(2,1)} async-done(((bf16[4,256,768]{2,0,1:T(4,128)(2,1)}), bf16[4,256,768]{2,0,1:T(4,128)(2,1)}, u32[]{:S(2)}, u32[]{:S(2)}) %all-to-all-start.2) | async-done | bytes 1572896 | tf_op jit(solution)/shard_map/all_to_all | solution.py:104
  155.6 2.8 copy.53
  158.3 4.7 %gather_fusion.4 = bf16[512,768]{1,0:T(8,128)(2,1)} fusion(bf16[1024,768]{1,0:T(8,128)(2,1)} %bitcast.52, s32[1024]{0:T(1024)S(1)} %pad_clamp_fusion), kind=kCustom, calls=%fused_computation.4 | custom fusion | bytes 1574912 | tf_op jit(solution)/shard_map/gather | solution.py:107
  163.0 2.2 gather.25
  165.2 2.8 reduce_sum.35
  168.0 4.2 %multiply_reduce_fusion = bf16[256,768]{1,0:T(8,128)(2,1)} fusion(f32[256,2,768]{2,1,0:T(2,128)} %reshape.206, f32[256,2]{1,0:T(8,128)S(1)} %copy.41), kind=kLoop, calls=%fused_computation.15 | loop fusion | flops 589824 | bytes 1968128 | tf_op jit(solution)/shard_map/reduce_sum | solution.py:108
  172.2 1.8 convert_element_type.88
  174.0 62.1 %reduce-scatter.6.cloned.1.call-done = bf16[4,96,384]{2,1,0:T(8,128)(2,1)} async-done(((bf16[4,768,384]{2,1,0:T(8,128)(2,1)}), bf16[4,96,384]{2,1,0:T(8,128)(2,1)}) %reduce-scatter.6.cloned.1.call-update) | async-done | bytes 294928 | tf_op jit(solution)/shard_map/reduce_scatter | solution.py:117
  236.2 1.8 convert_element_type.86
  238.0 70.5 %reduce-scatter.4.cloned.1.call-done = bf16[4,96,384]{2,1,0:T(8,128)(2,1)} async-done(((bf16[4,768,384]{2,1,0:T(8,128)(2,1)}), bf16[4,96,384]{2,1,0:T(8,128)(2,1)}) %reduce-scatter.4.cloned.1.call-update) | async-done | bytes 294928 | tf_op jit(solution)/shard_map/reduce_scatter | solution.py:114
  308.5 1.8 convert_element_type.84
  (36 shorter events, 0.3 us)
Async XLA Ops:
  7.2 80.0 %copy-start = (bf16[4,768,384]{2,1,0:T(8,128)(2,1)S(1)}, bf16[4,768,384]{2,1,0:T(8,128)(2,1)}, u32[]{:S(2)}) copy-start(bf16[4,768,384]{2,1,0:T(8,128)(2,1)} %param.11) | copy-start | bytes 7077892
  13.6 7.1 %copy-start.1 = (bf16[256,768]{1,0:T(8,128)(2,1)S(1)}, bf16[256,768]{1,0:T(8,128)(2,1)}, u32[]{:S(2)}) copy-start(bf16[256,768]{1,0:T(8,128)(2,1)} %param.10) | copy-start | bytes 1179652
  30.9 4.7 %copy-start.2 = (bf16[256,768]{1,0:T(8,128)(2,1)S(1)}, bf16[256,768]{1,0:T(8,128)(2,1)}, u32[]{:S(2)}) copy-start(bf16[256,768]{1,0:T(8,128)(2,1)} %param.7) | copy-start | bytes 1179652
  30.9 49.3 %all-to-all-start.1 = ((bf16[4,256,768]{2,0,1:T(4,128)(2,1)}), bf16[4,256,768]{2,0,1:T(4,128)(2,1)}, u32[]{:S(2)}, u32[]{:S(2)}) async-start(bf16[4,256,768]{2,0,1:T(4,128)(2,1)} %fusion), calls=%async_computation.1 | async-start | bytes 3145728 | tf_op jit(solution)/shard_map/all_to_all | solution.py:100
  35.4 136.8 %reduce-scatter.8.cloned.1.call-start = ((), (), s32[]{:S(2)}) async-start(), calls=%async_computation.8 | async-start | bytes 2654208 | tf_op jit(solution)/shard_map/reduce_scatter | solution.py:120
  42.4 5.6 %copy-start.4 = (bf16[1024,768]{1,0:T(8,128)(2,1)S(1)}, bf16[1024,768]{1,0:T(8,128)(2,1)}, u32[]{:S(2)}) copy-start(bf16[1024,768]{1,0:T(8,128)(2,1)} %gather_fusion) | copy-start | bytes 4718596
  43.2 20.5 %collective-permute-start = (bf16[1,4,64,768]{3,2,0,1:T(8,128)(2,1)}, bf16[1,4,64,768]{3,2,0,1:T(8,128)(2,1)}, u32[]{:S(2)}, u32[]{:S(2)}) collective-permute-start(bf16[1,4,64,768]{3,2,0,1:T(8,128)(2,1)} %get-tuple-element.12), channel_id=1, source_target_pairs={{0,1},{1,2},{2,3},{3,0},{4,5},{5,6},{6,7},{7,4},{8,9},{9,10},{10,1... | collective-permute-start | bytes 1179656 | tf_op jit(solution)/shard_map/ppermute | solution.py:95
  43.7 31.1 %collective-permute-start.2 = (bf16[1,4,64,768]{3,2,0,1:T(8,128)(2,1)S(1)}, bf16[1,4,64,768]{3,2,0,1:T(8,128)(2,1)}, u32[]{:S(2)}, u32[]{:S(2)}) collective-permute-start(bf16[1,4,64,768]{3,2,0,1:T(8,128)(2,1)S(1)} %get-tuple-element.10), channel_id=1, source_target_pairs={{0,3},{1,0},{2,1},{3,2},{4,7},{5,4},{6,5},{7,6},{8,11},{9,8},{10,9... | collective-permute-start | bytes 1179656 | tf_op jit(solution)/shard_map/ppermute | solution.py:95
  45.7 27.4 %collective-permute-start.1 = (bf16[1,4,64,768]{3,2,0,1:T(8,128)(2,1)S(1)}, bf16[1,4,64,768]{3,2,0,1:T(8,128)(2,1)}, u32[]{:S(2)}, u32[]{:S(2)}) collective-permute-start(bf16[1,4,64,768]{3,2,0,1:T(8,128)(2,1)S(1)} %get-tuple-element.11), channel_id=1, source_target_pairs={{0,2},{1,3},{2,0},{3,1},{4,6},{5,7},{6,4},{7,5},{8,10},{9,11},{10,... | collective-permute-start | bytes 1179656 | tf_op jit(solution)/shard_map/ppermute | solution.py:95
  49.4 27.2 %copy-start.5 = (bf16[4,768,384]{2,1,0:T(8,128)(2,1)S(1)}, bf16[4,768,384]{2,1,0:T(8,128)(2,1)}, u32[]{:S(2)}) copy-start(bf16[4,768,384]{2,1,0:T(8,128)(2,1)} %param.12) | copy-start | bytes 7077892
  83.9 3.3 %copy-start.3 = (bf16[4,4,64,768]{3,2,0,1:T(8,128)(2,1)S(1)}, bf16[4,4,64,768]{3,2,0,1:T(8,128)(2,1)}, u32[]{:S(2)}) copy-start(bf16[4,4,64,768]{3,2,0,1:T(8,128)(2,1)} %constant_dynamic-update-slice_fusion) | copy-start | bytes 4718596
  83.9 3.3 %copy-start.9 = (f32[4,256,384]{2,1,0:T(8,128)S(1)}, f32[4,256,384]{2,1,0:T(8,128)}, u32[]{:S(2)}) copy-start(f32[4,256,384]{2,1,0:T(8,128)} %fusion.14) | copy-start | bytes 4718596
  87.2 3.3 %copy-start.7 = (bf16[4,256,768]{1,2,0:T(8,128)(2,1)S(1)}, bf16[4,256,768]{1,2,0:T(8,128)(2,1)}, u32[]{:S(2)}) copy-start(bf16[4,256,768]{1,2,0:T(8,128)(2,1)} %copy.56) | copy-start | bytes 4718596
  89.6 1.0 copy-start.10
  93.0 143.2 %reduce-scatter.6.cloned.1.call-start = ((), (), s32[]{:S(2)}) async-start(), calls=%async_computation.7 | async-start | bytes 2654208 | tf_op jit(solution)/shard_map/reduce_scatter | solution.py:117
  97.3 211.2 %reduce-scatter.4.cloned.1.call-start = ((), (), s32[]{:S(2)}) async-start(), calls=%async_computation.6 | async-start | bytes 2654208 | tf_op jit(solution)/shard_map/reduce_scatter | solution.py:114
  106.6 24.5 %all-to-all-start = ((bf16[4,256,768]{2,0,1:T(4,128)(2,1)}), bf16[4,256,768]{2,0,1:T(4,128)(2,1)}, u32[]{:S(2)}, u32[]{:S(2)}) async-start(bf16[4,256,768]{2,0,1:T(4,128)(2,1)} %copy.46), calls=%async_computation | async-start | bytes 3145728 | tf_op jit(solution)/shard_map/all_to_all | solution.py:99
  111.0 1.7 copy-start.6
  111.0 1.9 copy-start.8
  131.1 24.5 %all-to-all-start.2 = ((bf16[4,256,768]{2,0,1:T(4,128)(2,1)}), bf16[4,256,768]{2,0,1:T(4,128)(2,1)}, u32[]{:S(2)}, u32[]{:S(2)}) async-start(bf16[4,256,768]{2,0,1:T(4,128)(2,1)} %copy.52), calls=%async_computation.2 | async-start | bytes 3145728 | tf_op jit(solution)/shard_map/all_to_all | solution.py:104
Sparse Core Ops, SparseCore 0:
  93.1 70.6 reduce-scatter.7
  167.3 68.8 reduce-scatter.5
  239.7 68.7 reduce-scatter.3
